TPU v7x, 32 devices: a whole 2x2x4 slice. The times are simulated.
32 devices in a mesh: src: 16 (over z, y, core), tgt: 2 (over x).
Axes of the slice: x: 2, y: 2, z: 4, core: 2. Of those that a mesh axis runs over, the one named last changes fastest.
Arguments:
- source_mean: float32 [16, 4096], P(None, 'src'), may hold values from -1 to 1, as said below
- target_points: float32 [16, 8192], P(None, 'tgt'), may hold values from -1 to 1
- precision: float32 [16], replicated, may hold values from 0.25 to 2, as said below
- target_values: float32 [8192, 128], P('tgt'), may hold values from 0.5 to 3
- cash: float32 [4096, 128], P('src'), may hold values from -3 to 3
- salvage: float32 [4096, 128], P('src'), may hold values from 0.5 to 3
- switch_cost: float32 [128], replicated, may hold values from 0.05 to 0.5
- cotangent: float32 [4096, 128], P('src'), may hold values from -0.5 to 1.5
- decision: int32 [4096, 128], P('src'), may hold values from 0 to 2
Outputs:
- source_value: float32 [4096, 128], P('src')
- target_adjoint: float32 [2, 4096, 128], P('tgt', 'src')
Inputs may be any that keep to these rules, and one draw needn't show every extreme that they name: `source_mean`: the first factor of source i lies between -1 + 2 i / 4096 and -1 + 2 (i + 1) / 4096. The first factor's precision is 1.5 or more.
All inputs are finite; a program needn't handle non-finite values.
Results may differ from a plain program's by a relative error of at most 0.00024.
Values sent between devices are 32-bit elements; how exact they have to be, the bound alone decides.
No kernel may reach another device: no remote copies, remote signals or barrier semaphores. Data moves between devices by JAX's collectives and lax.ppermute only.
A program may use at most 64 MiB of HBM per device.

v0:
```python
import jax
import jax.numpy as jnp
from jax import lax
from jax.sharding import PartitionSpec as P


def choose_value(continuation, cash_part, salvage_part, cost_part):
    hold_value = continuation + cash_part
    paired = hold_value.reshape(hold_value.shape[0], -1, 2)[:, :, ::-1].reshape(hold_value.shape)
    switched = paired - cost_part[None, :]
    return jnp.maximum(jnp.maximum(hold_value, switched), salvage_part)


def adjoint_input(cotangent, decision):
    held = jnp.where(decision == 0, cotangent, 0.0)
    moved = jnp.where(decision == 1, cotangent, 0.0)
    swapped = moved.reshape(moved.shape[0], -1, 2)[:, :, ::-1].reshape(moved.shape)
    return held + swapped


def transposed_product(left_part, right_part):
    return lax.dot_general(
        left_part,
        right_part,
        (((0,), (0,)), ((), ())),
        precision=lax.Precision.HIGHEST,
        preferred_element_type=jnp.float32,
    )


def on_device(
    source_mean,
    target_points,
    precision,
    target_values,
    cash,
    salvage,
    switch_cost,
    cotangent,
    decision,
):
    source_total = source_mean.shape[1] * lax.axis_size("src")
    target_total = target_points.shape[1] * lax.axis_size("tgt")
    scaled = source_mean * precision[:, None]
    offset = -0.5 * jnp.sum(scaled * source_mean, axis=0)
    density = jnp.exp(transposed_product(scaled, target_points) + offset[:, None])
    column_sum = lax.psum(jnp.sum(density, axis=0), "src")
    factor = source_total / target_total / column_sum
    scaled_values = target_values * factor[:, None]
    partial_terms = jnp.dot(
        density, scaled_values, precision=lax.Precision.HIGHEST, preferred_element_type=jnp.float32
    )
    continuation = lax.psum(partial_terms, "tgt")
    source_value = choose_value(continuation, cash, salvage, switch_cost)
    adjoint_in = adjoint_input(cotangent, decision)
    row_count = target_points.shape[1] // lax.axis_size("src")
    weights = density * factor[None, :]
    weighted_terms = transposed_product(weights, adjoint_in)
    own_rows = lax.psum_scatter(weighted_terms, "src", scatter_dimension=0, tiled=True)
    target_adjoint = own_rows.reshape(1, row_count, own_rows.shape[1])
    return (source_value, target_adjoint)


def solution(mesh):
    placed = (
        P(None, "src"),
        P(None, "tgt"),
        P(),
        P("tgt", None),
        P("src", None),
        P("src", None),
        P(),
        P("src", None),
        P("src", None),
    )
    return jax.shard_map(
        on_device,
        mesh=mesh,
        in_specs=placed,
        out_specs=(P("src", None), P("tgt", "src", None)),
        check_vma=False,
    )
```

profile of v0, /device:TPU:0, one launch (start us, length us, event | category | flops | bytes accessed | tf_op | source)
XLA Modules:
  0.0 162.9 jit_solution(15656077067644059108)
XLA Ops:
  8.0 0.0 copy-start
  8.0 0.0 copy-start.1
  8.0 0.0 all-reduce.2.cloned.1.call-start
  8.1 1.0 fusion.13
  9.0 0.0 copy-done
  9.0 6.3 %fusion.17 = (f32[4096]{0:T(1024)S(1)}, f32[256,4096]{1,0:T(8,128)}) fusion(f32[256]{0:T(256)S(1)} %broadcast_multiply_fusion, f32[16,4096]{1,0:T(8,128)S(1)} %copy-done, f32[16,256]{1,0:T(8,128)} %param.9, f32[16]{0:T(128)} %param.11), kind=kOutput, calls=%fused_computation.23 | convolution fusion | flops 203423744 | bytes 4490304 | tf_op jit(solution)/shard_map/dot_general | solution.py:22
  15.4 63.1 %psum.14 = f32[4096]{0:T(1024)S(1)} all-reduce(f32[4096]{0:T(1024)S(1)} %get-tuple-element.2), channel_id=1, replica_groups=mesh['src'=16,'tgt'=2] {'src'}, use_global_device_ids=true, to_apply=%region_2.0 | all-reduce | flops 4096 | bytes 32768 | tf_op jit(solution)/shard_map/psum | solution.py:47
  78.5 0.0 copy-done.1
  78.5 6.4 %fusion.4 = f32[256,128]{1,0:T(8,128)} fusion(f32[256,4096]{1,0:T(8,128)} %get-tuple-element.3, f32[4096,128]{1,0:T(8,128)S(1)} %copy-done.1, f32[4096]{0:T(1024)S(1)} %broadcast_divide_fusion), kind=kOutput, calls=%fused_computation.5 | convolution fusion | flops 1611137024 | bytes 6438912 | tf_op jit(solution)/shard_map/dot_general | solution.py:50
  84.9 0.0 all-reduce.2.cloned.1.call-update
  84.9 0.2 reduce-scatter.2.cloned.1.call-start
  85.1 0.0 copy-done.4
  85.1 0.1 copy.14
  85.2 0.1 copy.13
  85.4 0.1 reshape.28
  85.4 0.4 rev.7
  85.8 0.1 reshape.29
  85.9 0.0 copy-start.2
  86.0 0.0 copy-start.3
  86.0 0.0 copy-start.6
  86.0 10.3 %fusion.1 = f32[4096,128]{1,0:T(8,128)} fusion(f32[256,4096]{1,0:T(8,128)} %get-tuple-element.3, f32[4096]{0:T(1024)S(1)} %broadcast_divide_fusion, f32[256,128]{0,1:T(8,128)S(1)} %reshape.29, f32[256,128]{0,1:T(8,128)S(1)} %copy.14, s32[256,128]{0,1:T(8,128)S(1)} %copy.13), kind=kOutput, calls=%fused_computation.2 | convolution fusion | flops 1611759616 | bytes 6701056 | tf_op jit(solution)/shard_map/dot_general | solution.py:22
  96.3 0.0 reduce-scatter.2.cloned.1.call-update
  96.3 7.5 %all-reduce.2.cloned.1.call-done = f32[256,128]{1,0:T(8,128)} async-done(((f32[256,128]{1,0:T(8,128)}), f32[256,128]{1,0:T(8,128)}) %all-reduce.2.cloned.1.call-update) | async-done | bytes 131088 | tf_op jit(solution)/shard_map/psum | solution.py:53
  103.8 0.0 copy-done.2
  103.8 0.9 add.22
  104.8 0.1 copy.11
  104.9 0.1 reshape.26
  104.9 0.4 rev.6
  105.3 0.1 reshape.27
  105.4 0.1 copy.12
  105.6 0.7 maximum_maximum_fusion
  106.2 49.2 %reduce-scatter.2.cloned.1.call-done = f32[256,128]{1,0:T(8,128)} async-done(((f32[4096,128]{1,0:T(8,128)}), f32[256,128]{1,0:T(8,128)}) %reduce-scatter.2.cloned.1.call-update) | async-done | bytes 131088 | tf_op jit(solution)/shard_map/reduce_scatter | solution.py:59
  (8 shorter events, 0.0 us)
Async XLA Ops:
  8.0 1.0 copy-start
  8.0 70.5 %copy-start.1 = (f32[4096,128]{1,0:T(8,128)S(1)}, f32[4096,128]{1,0:T(8,128)}, u32[]{:S(2)}) copy-start(f32[4096,128]{1,0:T(8,128)} %param.12) | copy-start | bytes 6291460
  8.0 95.8 %all-reduce.2.cloned.1.call-start = ((), (), s32[]{:S(2)}) async-start(), calls=%async_computation.1 | async-start | bytes 262144 | tf_op jit(solution)/shard_map/psum | solution.py:53
  15.4 69.7 %copy-start.4 = (f32[256,128]{1,0:T(8,128)S(1)}, f32[256,128]{1,0:T(8,128)}, u32[]{:S(2)}) copy-start(f32[256,128]{1,0:T(8,128)} %param.16) | copy-start | bytes 393220
  15.4 69.9 %copy-start.5 = (s32[256,128]{1,0:T(8,128)S(1)}, s32[256,128]{1,0:T(8,128)}, u32[]{:S(2)}) copy-start(s32[256,128]{1,0:T(8,128)} %param.17) | copy-start | bytes 393220
  84.9 70.5 %reduce-scatter.2.cloned.1.call-start = ((), (), s32[]{:S(2)}) async-start(), calls=%async_computation.2 | async-start | bytes 2228224 | tf_op jit(solution)/shard_map/reduce_scatter | solution.py:59
  85.9 17.9 %copy-start.2 = (f32[256,128]{1,0:T(8,128)S(1)}, f32[256,128]{1,0:T(8,128)}, u32[]{:S(2)}) copy-start(f32[256,128]{1,0:T(8,128)} %param.13) | copy-start | bytes 393220
  86.0 19.6 %copy-start.3 = (f32[256,128]{1,0:T(8,128)S(1)}, f32[256,128]{1,0:T(8,128)}, u32[]{:S(2)}) copy-start(f32[256,128]{1,0:T(8,128)} %param.14) | copy-start | bytes 393220
  86.0 19.6 %copy-start.6 = (f32[128]{0:T(128)S(1)}, f32[128]{0:T(128)}, u32[]{:S(2)}) copy-start(f32[128]{0:T(128)} %param.15) | copy-start | bytes 1540
Sparse Core Ops, SparseCore 0:
  85.0 18.7 all-reduce.1
Sparse Core Ops, SparseCore 1:
  96.4 59.0 reduce-scatter.1
where the time goes:
time: 163 us
  blocking collectives  63.1 us (39%)
  waiting for transfers between devices  56.7 us (35%)
  matrix products  23 us (14%)
  between operations  15.6 us (10%)
  other arithmetic  2.59 us (2%)
    psum x1, blocking collectives, on_device(): column_sum = lax.psum(jnp.sum(density, axis=0), 'src')  63.1 us
    reduce_scatter x1, waiting for transfers between devices, on_device(): lax.psum_scatter(weighted_terms, 'src', scatter_dimension=0, tiled=True)  49.2 us
    dot_general x2, matrix products, transposed_product(): lax.dot_general(left_part, right_part, (((0,), (0,)), ((), ())), precisio...  16.6 us
    psum x1, waiting for transfers between devices, on_device(): continuation = lax.psum(partial_terms, 'tgt')  7.53 us
    dot_general x1, matrix products, on_device(): jnp.dot(density, scaled_values, precision=lax.Precision.HIGHEST, preferre...  6.36 us
  transfers between devices with their start and end apart: 2, of which 2 were waited for; matrix products, arithmetic and copies ran while one was open for 8% of the time, Pallas kernels for 0%

commit v1 on v0

--- a/solution.py
+++ b/solution.py
@@ -44,7 +44,7 @@
     scaled = source_mean * precision[:, None]
     offset = -0.5 * jnp.sum(scaled * source_mean, axis=0)
     density = jnp.exp(transposed_product(scaled, target_points) + offset[:, None])
-    column_sum = lax.psum(jnp.sum(density, axis=0), "src")
+    column_sum = jnp.sum(lax.all_gather(jnp.sum(density, axis=0), "src"), axis=0)
     factor = source_total / target_total / column_sum
     scaled_values = target_values * factor[:, None]
     partial_terms = jnp.dot(

time: 163 us -> 124 us (0.76)
  blocking collectives: 63.1 us -> 23.9 us
    psum x1 -> x0, blocking collectives: 63.1 us -> none  [on_device(): column_sum = lax.psum(jnp.sum(density, axis=0), 'src')]
    all_gather x0 -> x1, blocking collectives: none -> 23.9 us  [on_device(): lax.all_gather(jnp.sum(density, axis=0), 'src')]
  transfers between devices with their start and end apart: 2 -> 2, of which waited for: 2 -> 2; matrix products, arithmetic and copies ran while one was open for 8% -> 11% of each run, Pallas kernels for 0% -> 0%
where the time goes in v1:
time: 124 us
  waiting for transfers between devices  56.8 us (46%)
  blocking collectives  23.9 us (19%)
  matrix products  23 us (19%)
  between operations  15.7 us (13%)
  other arithmetic  2.63 us (2%)
  local copies, waits for them, and re-layouts  1.57 us (1%)
    reduce_scatter x1, waiting for transfers between devices, on_device(): lax.psum_scatter(weighted_terms, 'src', scatter_dimension=0, tiled=True)  49.2 us
    all_gather x1, blocking collectives, on_device(): lax.all_gather(jnp.sum(density, axis=0), 'src')  23.9 us
    dot_general x2, matrix products, transposed_product(): lax.dot_general(left_part, right_part, (((0,), (0,)), ((), ())), precisio...  16.6 us
    psum x1, waiting for transfers between devices, on_device(): continuation = lax.psum(partial_terms, 'tgt')  7.55 us
    dot_general x1, matrix products, on_device(): jnp.dot(density, scaled_values, precision=lax.Precision.HIGHEST, preferre...  6.36 us
  transfers between devices with their start and end apart: 2, of which 2 were waited for; matrix products, arithmetic and copies ran while one was open for 11% of the time, Pallas kernels for 0%

profile of v1, /device:TPU:0, one launch (start us, length us, event | category | flops | bytes accessed | tf_op | source)
XLA Modules:
  0.0 123.9 jit_solution(14371811364679077281)
XLA Ops:
  8.0 0.0 copy-start
  8.0 0.0 copy-start.1
  8.0 0.0 all-reduce.2.cloned.1.call-start
  8.1 1.0 fusion.13
  9.0 0.0 copy-done
  9.0 6.3 %fusion.17 = (f32[4096]{0:T(1024)S(1)}, f32[256,4096]{1,0:T(8,128)}) fusion(f32[256]{0:T(256)S(1)} %broadcast_multiply_fusion, f32[16,4096]{1,0:T(8,128)S(1)} %copy-done, f32[16,256]{1,0:T(8,128)} %param.9, f32[16]{0:T(128)} %param.11), kind=kOutput, calls=%fused_computation.23 | convolution fusion | flops 203423744 | bytes 4490304 | tf_op jit(solution)/shard_map/dot_general | solution.py:22
  15.4 23.9 %all-gather = f32[65536]{0:T(1024)S(1)} all-gather(f32[4096]{0:T(1024)S(1)} %get-tuple-element.2), channel_id=2, replica_groups=mesh['src'=16,'tgt'=2] {'src'}, dimensions={0}, use_global_device_ids=true | all-gather | bytes 278528 | tf_op jit(solution)/shard_map/all_gather | solution.py:47
  39.3 0.1 reshape.35
  39.4 0.0 copy-done.1
  39.4 6.4 %fusion.4 = f32[256,128]{1,0:T(8,128)} fusion(f32[256,4096]{1,0:T(8,128)} %get-tuple-element.3, f32[4096,128]{1,0:T(8,128)S(1)} %copy-done.1, f32[4096]{0:T(1024)S(1)} %broadcast_divide_fusion), kind=kOutput, calls=%fused_computation.5 | convolution fusion | flops 1611137024 | bytes 6438912 | tf_op jit(solution)/shard_map/dot_general | solution.py:50
  45.8 0.0 all-reduce.2.cloned.1.call-update
  45.8 0.2 reduce-scatter.2.cloned.1.call-start
  46.1 0.0 copy-done.4
  46.1 0.1 copy.26
  46.2 0.1 copy.25
  46.3 0.1 reshape.32
  46.4 0.4 rev.7
  46.8 0.1 reshape.33
  46.9 0.0 copy-start.2
  46.9 0.0 copy-start.3
  46.9 0.0 copy-start.6
  46.9 10.3 %fusion.1 = f32[4096,128]{1,0:T(8,128)} fusion(f32[256,4096]{1,0:T(8,128)} %get-tuple-element.3, f32[4096]{0:T(1024)S(1)} %broadcast_divide_fusion, f32[256,128]{0,1:T(8,128)S(1)} %reshape.33, f32[256,128]{0,1:T(8,128)S(1)} %copy.26, s32[256,128]{0,1:T(8,128)S(1)} %copy.25), kind=kOutput, calls=%fused_computation.2 | convolution fusion | flops 1611759616 | bytes 6701056 | tf_op jit(solution)/shard_map/dot_general | solution.py:22
  57.2 0.0 reduce-scatter.2.cloned.1.call-update
  57.3 7.5 %all-reduce.2.cloned.1.call-done = f32[256,128]{1,0:T(8,128)} async-done(((f32[256,128]{1,0:T(8,128)}), f32[256,128]{1,0:T(8,128)}) %all-reduce.2.cloned.1.call-update) | async-done | bytes 131088 | tf_op jit(solution)/shard_map/psum | solution.py:53
  64.8 0.9 add.20
  65.7 0.1 copy.23
  65.8 0.1 reshape.30
  65.9 0.4 rev.6
  66.3 0.1 reshape.31
  66.4 0.1 copy.24
  66.5 0.7 maximum_maximum_fusion
  67.2 49.2 %reduce-scatter.2.cloned.1.call-done = f32[256,128]{1,0:T(8,128)} async-done(((f32[4096,128]{1,0:T(8,128)}), f32[256,128]{1,0:T(8,128)}) %reduce-scatter.2.cloned.1.call-update) | async-done | bytes 131088 | tf_op jit(solution)/shard_map/reduce_scatter | solution.py:59
  (10 shorter events, 0.1 us)
Async XLA Ops:
  8.0 1.0 copy-start
  8.0 31.4 %copy-start.1 = (f32[4096,128]{1,0:T(8,128)S(1)}, f32[4096,128]{1,0:T(8,128)}, u32[]{:S(2)}) copy-start(f32[4096,128]{1,0:T(8,128)} %param.12) | copy-start | bytes 6291460
  8.0 56.8 %all-reduce.2.cloned.1.call-start = ((), (), s32[]{:S(2)}) async-start(), calls=%async_computation.1 | async-start | bytes 262144 | tf_op jit(solution)/shard_map/psum | solution.py:53
  15.4 30.7 %copy-start.4 = (f32[256,128]{1,0:T(8,128)S(1)}, f32[256,128]{1,0:T(8,128)}, u32[]{:S(2)}) copy-start(f32[256,128]{1,0:T(8,128)} %param.16) | copy-start | bytes 393220
  15.4 30.8 %copy-start.5 = (s32[256,128]{1,0:T(8,128)S(1)}, s32[256,128]{1,0:T(8,128)}, u32[]{:S(2)}) copy-start(s32[256,128]{1,0:T(8,128)} %param.17) | copy-start | bytes 393220
  45.8 70.6 %reduce-scatter.2.cloned.1.call-start = ((), (), s32[]{:S(2)}) async-start(), calls=%async_computation.2 | async-start | bytes 2228224 | tf_op jit(solution)/shard_map/reduce_scatter | solution.py:59
  46.9 17.9 %copy-start.2 = (f32[256,128]{1,0:T(8,128)S(1)}, f32[256,128]{1,0:T(8,128)}, u32[]{:S(2)}) copy-start(f32[256,128]{1,0:T(8,128)} %param.13) | copy-start | bytes 393220
  46.9 19.6 %copy-start.3 = (f32[256,128]{1,0:T(8,128)S(1)}, f32[256,128]{1,0:T(8,128)}, u32[]{:S(2)}) copy-start(f32[256,128]{1,0:T(8,128)} %param.14) | copy-start | bytes 393220
  46.9 19.6 %copy-start.6 = (f32[128]{0:T(128)S(1)}, f32[128]{0:T(128)}, u32[]{:S(2)}) copy-start(f32[128]{0:T(128)} %param.15) | copy-start | bytes 1540
Sparse Core Ops, SparseCore 0:
  46.0 18.8 all-reduce.1
Sparse Core Ops, SparseCore 1:
  57.3 59.0 reduce-scatter.1
